TPU v7x, 32 devices: a whole 2x2x4 slice. The times are simulated.
32 devices in a mesh: groups: 2 (over x), frame: 8 (over z, y), space: 2 (over core).
Axes of the slice: x: 2, y: 2, z: 4, core: 2. Of those that a mesh axis runs over, the one named last changes fastest.
Arguments:
- queries: bfloat16 [16, 12, 80, 2240], P(('groups', 'frame'), 'space'), parts along dimension 0, may hold values from -6 to 6
- keys: bfloat16 [16, 12, 80, 2240], P(('groups', 'frame'), 'space'), parts along dimension 0, may hold values from -6 to 6
- values: bfloat16 [16, 12, 80, 2240], P(('groups', 'frame'), 'space'), parts along dimension 0, may hold values from -6 to 6
- residual: bfloat16 [16, 12, 80, 2240], P(('groups', 'frame'), 'space'), parts along dimension 0, may hold values from -6 to 6
- attn_gain: float32 [2240], replicated, may hold values from 0.5 to 1.5
- value_taps: float32 [9, 2240], replicated, may hold values from -2 to 2
- gate_taps: float32 [9, 2240], replicated, may hold values from -2 to 2
Outputs:
- block_out: bfloat16 [16, 12, 80, 2240], P(('groups', 'frame'), 'space'), parts along dimension 0
There are 2 independent parts, one for each index of `groups`. A program takes and returns all parts, laid end to end along the dimension named above; an argument that names none is the same for every part. Nothing has to cross between parts.
All inputs are finite; a program needn't handle non-finite values.
Results may differ from a plain program's by a relative error of at most 0.008.
Values may be sent and summed in bfloat16 or wider, within the bound.
A program may use at most 128 MiB of HBM per device.

v0:
```python
import jax
import jax.numpy as jnp
from jax import lax
from jax.sharding import PartitionSpec as P

HEAD_DIM = 112


def entering(value, axis, combine, identity):
    devices, here = (lax.axis_size(axis), lax.axis_index(axis))
    everything = lax.all_gather(value.astype(jnp.bfloat16), axis)
    start = jnp.broadcast_to(jnp.asarray(identity, value.dtype), value.shape)

    def step(k, before):
        reached = k < here
        new = combine(before, everything[k].astype(value.dtype))
        return jnp.where(reached, new, before)

    return lax.fori_loop(0, devices, step, start)


def with_halo(value, sides, width):
    for axis, dim in sides:
        devices, length = (lax.axis_size(axis), value.shape[dim])
        up = [(i, (i + 1) % devices) for i in range(devices - 1)]
        down = [(j, i) for i, j in up]
        last = lax.slice_in_dim(value, length - width, length, axis=dim)
        initial = lax.slice_in_dim(value, 0, width, axis=dim)
        before = lax.ppermute(last, axis, up)
        after = lax.ppermute(initial, axis, down)
        value = jnp.concatenate([before, value, after], axis=dim)
    return value


def add_states(earlier, later):
    return earlier + later


def on_device(queries, keys, values, residual, attn_gain, value_taps, gate_taps):
    frames, rows, width, dim = queries.shape
    heads = dim // HEAD_DIM
    tokens = frames * rows * width
    feature_keys = jnp.maximum(keys, 0).reshape(tokens, heads, HEAD_DIM)
    value_rows = values.reshape(tokens, heads, HEAD_DIM)
    partial_value_state = jnp.einsum(
        "rag,rap->agp", feature_keys, value_rows, preferred_element_type=jnp.float32
    )
    share = lax.psum_scatter(
        partial_value_state.astype(jnp.bfloat16), "space", scatter_dimension=0, tiled=True
    ).astype(jnp.float32)
    prev_share = entering(share, "frame", add_states, jnp.zeros_like(share))
    previous_frame_pass, local_frame_pass = (
        lax.all_gather(prev_share.astype(jnp.bfloat16), "space", axis=0, tiled=True),
        lax.all_gather(share.astype(jnp.bfloat16), "space", axis=0, tiled=True),
    )
    feature_queries = jnp.maximum(queries, 0).reshape(tokens, heads, HEAD_DIM)
    numerator_sum = jnp.einsum(
        "ubq,bql->ubl", feature_queries, local_frame_pass, preferred_element_type=jnp.float32
    )
    numerator_sum = numerator_sum + jnp.einsum(
        "ubq,bql->ubl", feature_queries, previous_frame_pass, preferred_element_type=jnp.float32
    )
    scale = lax.rsqrt(jnp.mean(numerator_sum * numerator_sum, axis=-1, keepdims=True) + 1e-06)
    normed = (numerator_sum * scale).reshape(rows, width, dim)
    mixed = (residual.reshape(rows, width, dim).astype(jnp.float32) + normed * attn_gain).astype(
        jnp.bfloat16
    )
    extended = with_halo(mixed, (("space", 0),), 1)
    padded = jnp.pad(extended.astype(jnp.float32), ((0, 0), (1, 1), (0, 0)))
    conv_v = jnp.zeros((rows, width, dim), jnp.float32)
    conv_g = jnp.zeros((rows, width, dim), jnp.float32)
    for tap_row in range(3):
        for tap_col in range(3):
            window = padded[tap_row : tap_row + rows, tap_col : tap_col + width, :]
            conv_v = conv_v + value_taps[3 * tap_row + tap_col] * window
            conv_g = conv_g + gate_taps[3 * tap_row + tap_col] * window
    block_out = mixed.astype(jnp.float32) + conv_v * jax.nn.silu(conv_g)
    return block_out.astype(jnp.bfloat16).reshape(frames, rows, width, dim)


def solution(mesh):
    placed = (
        P(("groups", "frame"), "space", None, None),
        P(("groups", "frame"), "space", None, None),
        P(("groups", "frame"), "space", None, None),
        P(("groups", "frame"), "space", None, None),
        P(),
        P(),
        P(),
    )
    return jax.shard_map(
        on_device,
        mesh=mesh,
        in_specs=placed,
        out_specs=P(("groups", "frame"), "space", None, None),
        check_vma=False,
    )
```

profile of v0, /device:TPU:0, one launch (start us, length us, event | category | flops | bytes accessed | tf_op | source)
XLA Modules:
  0.0 145.3 jit_solution(8434362103516767503)
XLA Ops:
  6.5 0.0 reduce-scatter.2.cloned.1.call-start
  6.5 1.8 %broadcast_maximum_fusion.1 = bf16[1,6,80,2240]{3,2,1,0:T(8,128)(2,1)S(1)} fusion(bf16[1,6,80,2240]{3,2,1,0:T(8,128)(2,1)} %param.10), kind=kLoop, calls=%fused_computation.21 | loop fusion | flops 1075200 | bytes 4300800 | tf_op jit(solution)/shard_map/max | solution.py:43
  8.3 4.1 %reshape.47 = bf16[480,20,112]{2,1,0:T(8,128)(2,1)} reshape(bf16[1,6,80,2240]{3,2,1,0:T(8,128)(2,1)S(1)} %broadcast_maximum_fusion.1) | data formatting | bytes 4300800 | tf_op jit(solution)/shard_map/reshape | solution.py:43
  12.4 0.0 copy-start
  12.4 6.3 %reshape.48 = bf16[480,20,112]{2,1,0:T(8,128)(2,1)} reshape(bf16[1,6,80,2240]{3,2,1,0:T(8,128)(2,1)} %param.11) | data formatting | bytes 4300800 | tf_op jit(solution)/shard_map/reshape | solution.py:44
  18.8 0.0 copy-done
  18.8 3.8 %fusion.6 = bf16[20,112,112]{2,1,0:T(8,128)(2,1)} fusion(bf16[480,20,112]{2,1,0:T(8,128)(2,1)} %reshape.48, bf16[480,20,112]{2,1,0:T(8,128)(2,1)S(1)} %copy-done), kind=kOutput, calls=%fused_computation.19 | convolution fusion | flops 241095680 | bytes 4802560 | tf_op jit(solution)/shard_map/rag,rap->agp/dot_general | solution.py:45
  22.5 0.0 reduce-scatter.2.cloned.1.call-update
  22.6 0.0 all-gather.3.cloned.1.call-start
  22.6 10.8 %reduce-scatter.2.cloned.1.call-done = bf16[10,112,112]{2,1,0:T(8,128)(2,1)} async-done(((bf16[20,112,112]{2,1,0:T(8,128)(2,1)}), bf16[10,112,112]{2,1,0:T(8,128)(2,1)}) %reduce-scatter.2.cloned.1.call-update) | async-done | bytes 250896 | tf_op jit(solution)/shard_map/reduce_scatter | solution.py:48
  33.4 0.0 all-gather.3.cloned.1.call-update
  33.4 1.8 %broadcast_maximum_fusion = bf16[1,6,80,2240]{3,2,1,0:T(8,128)(2,1)S(1)} fusion(bf16[1,6,80,2240]{3,2,1,0:T(8,128)(2,1)} %param.9), kind=kLoop, calls=%fused_computation.20 | loop fusion | flops 1075200 | bytes 4300800 | tf_op jit(solution)/shard_map/max | solution.py:56
  35.2 0.0 copy-start.2
  35.2 4.1 %reshape.49 = bf16[480,20,112]{2,1,0:T(8,128)(2,1)} reshape(bf16[1,6,80,2240]{3,2,1,0:T(8,128)(2,1)S(1)} %broadcast_maximum_fusion) | data formatting | bytes 4300800 | tf_op jit(solution)/shard_map/reshape | solution.py:56
  39.4 3.6 %copy.25 = bf16[480,20,112]{0,2,1:T(8,128)(2,1)S(1)} copy(bf16[480,20,112]{2,1,0:T(8,128)(2,1)} %reshape.49) | data formatting | bytes 4300800 | tf_op jit(solution)/shard_map/reshape | solution.py:56
  42.9 0.0 copy-done.2
  42.9 2.2 %all_gather.12 = bf16[20,112,112]{2,1,0:T(8,128)(2,1)S(1)} all-gather(bf16[10,112,112]{2,1,0:T(8,128)(2,1)S(1)} %copy-done.2), channel_id=1, replica_groups=mesh['groups'=2,'frame'=8,'space'=2] {'space'}, dimensions={0}, use_global_device_ids=true | all-gather | bytes 752640 | tf_op jit(solution)/shard_map/all_gather | solution.py:54
  45.2 2.9 %fusion.12 = f32[20,112,480]{2,1,0:T(8,128)} fusion(bf16[20,112,112]{2,1,0:T(8,128)(2,1)S(1)} %all_gather.12, bf16[480,20,112]{0,2,1:T(8,128)(2,1)S(1)} %copy.25), kind=kOutput, calls=%fused_computation.42 | convolution fusion | flops 240844800 | bytes 6952960 | tf_op jit(solution)/shard_map/ubq,bql->ubl/dot_general | solution.py:57
  48.0 39.8 %all-gather.3.cloned.1.call-done = bf16[80,112,112]{2,1,0:T(8,128)(2,1)} async-done(((bf16[10,112,112]{2,1,0:T(8,128)(2,1)}), bf16[80,112,112]{2,1,0:T(8,128)(2,1)}) %all-gather.3.cloned.1.call-update) | async-done | bytes 2007056 | tf_op jit(solution)/shard_map/all_gather | solution.py:11
  87.8 10.1 %while.14 = (s32[]{:T(128)}, f32[10,112,112]{2,1,0:T(8,128)S(1)}, s32[]{:T(128)}, bf16[8,10,112,112]{3,2,1,0:T(8,128)(2,1)}, s32[]{:T(128)}, /*index=5*/s32[]{:T(128)}) while((s32[]{:T(128)}, f32[10,112,112]{2,1,0:T(8,128)S(1)}, s32[]{:T(128)}, bf16[8,10,112,112]{3,2,1,0:T(8,128)(2,1)}, s32[]{:T(128)}, /*index=5*/s32[]{:T(128)}) %tuple.66), condition=%wide.region_2.3_spmd.clone, body=%wide.region_1.2_spmd.clone.sunk | while | flops 501764 | bytes 1254493 | solution.py:19
  87.8 1.2 add_select_fusion.2
  89.0 1.2 add_select_fusion.2
  90.3 1.2 add_select_fusion.2
  91.6 1.2 add_select_fusion.2
  92.8 1.2 add_select_fusion.2
  94.1 1.2 add_select_fusion.2
  95.4 1.2 add_select_fusion.2
  96.7 1.2 add_select_fusion.2
  98.0 2.2 %all_gather.15 = bf16[20,112,112]{2,1,0:T(8,128)(2,1)S(1)} all-gather(bf16[10,112,112]{2,1,0:T(8,128)(2,1)S(1)} %convert_element_type.42), channel_id=1, replica_groups=mesh['groups'=2,'frame'=8,'space'=2] {'space'}, dimensions={0}, use_global_device_ids=true | all-gather | bytes 752640 | tf_op jit(solution)/shard_map/all_gather | solution.py:53
  100.2 3.2 %fusion = (f32[480,20]{0,1:T(8,128)S(1)}, f32[20,112,480]{2,1,0:T(8,128)S(1)}) fusion(f32[20,112,480]{2,1,0:T(8,128)} %fusion.12, bf16[20,112,112]{2,1,0:T(8,128)(2,1)S(1)} %all_gather.15, bf16[480,20,112]{0,2,1:T(8,128)(2,1)S(1)} %copy.25), kind=kOutput, calls=%fused_computation.9 | convolution fusion | flops 244060800 | bytes 11292160 | tf_op jit(solution)/shard_map/ubq,bql->ubl/dot_general | solution.py:60
  103.4 2.9 %bitcast_multiply_fusion = f32[480,20,112]{0,2,1:T(8,128)} fusion(f32[20,112,480]{2,1,0:T(8,128)S(1)} %get-tuple-element.129, f32[480,20]{0,1:T(8,128)S(1)} %add_rsqrt_fusion), kind=kLoop, calls=%fused_computation.7 | loop fusion | flops 1075200 | bytes 8640000 | tf_op jit(solution)/shard_map/mul | solution.py:64
  106.3 6.1 %copy.28 = f32[480,20,112]{2,1,0:T(8,128)} copy(f32[480,20,112]{0,2,1:T(8,128)} %bitcast_multiply_fusion) | data formatting | bytes 8601600 | tf_op jit(solution)/shard_map/mul | solution.py:64
  112.4 0.0 copy-start.1
  112.4 0.0 copy-start.5
  112.4 7.0 %reshape.50 = f32[6,80,2240]{2,1,0:T(8,128)} reshape(f32[480,20,112]{2,1,0:T(8,128)} %copy.28) | data formatting | bytes 8601600 | tf_op jit(solution)/shard_map/reshape | solution.py:64
  119.4 0.0 copy-done.1
  119.4 0.0 copy-done.5
  119.4 0.0 copy-start.3
  119.4 0.0 copy-start.4
  119.4 2.8 %fusion.1 = bf16[6,80,2240]{2,1,0:T(8,128)(2,1)S(1)} fusion(f32[6,80,2240]{2,1,0:T(8,128)} %reshape.50, bf16[1,6,80,2240]{3,2,1,0:T(8,128)(2,1)S(1)} %copy-done.1, f32[2240]{0:T(1024)S(1)} %copy-done.5), kind=kLoop, calls=%fused_computation.11 | loop fusion | flops 4300800 | bytes 8610560 | tf_op jit(solution)/shard_map/convert_element_type | solution.py:65
  122.2 0.1 fusion.11
  122.3 2.1 %collective-permute-start = (bf16[1,80,2240]{2,1,0:T(8,128)(2,1)S(1)}, bf16[1,80,2240]{2,1,0:T(8,128)(2,1)S(1)}, u32[]{:S(2)}, u32[]{:S(2)}) collective-permute-start(bf16[1,80,2240]{2,1,0:T(8,128)(2,1)S(1)} %get-tuple-element.126), channel_id=1, source_target_pairs={{0,1},{2,3},{4,5},{6,7},{8,9},{10,11},{12,13},{14,15},{16,17},{18,... | collective-permute-start | bytes 1075208 | tf_op jit(solution)/shard_map/ppermute | solution.py:29
  124.4 1.5 %collective-permute-start.1 = (bf16[1,80,2240]{2,1,0:T(8,128)(2,1)S(1)}, bf16[1,80,2240]{2,1,0:T(8,128)(2,1)S(1)}, u32[]{:S(2)}, u32[]{:S(2)}) collective-permute-start(bf16[1,80,2240]{2,1,0:T(8,128)(2,1)S(1)} %get-tuple-element.127), channel_id=1, source_target_pairs={{1,0},{3,2},{5,4},{7,6},{9,8},{11,10},{13,12},{15,14},{17,16},{19,... | collective-permute-start | bytes 1075208 | tf_op jit(solution)/shard_map/ppermute | solution.py:30
  125.8 0.0 copy-done.3
  125.9 0.0 copy-done.4
  125.9 0.4 slice_reduce_fusion.8
  126.3 0.0 collective-permute-done
  126.3 1.6 %collective-permute-done.1 = bf16[1,80,2240]{2,1,0:T(8,128)(2,1)S(1)} collective-permute-done((bf16[1,80,2240]{2,1,0:T(8,128)(2,1)S(1)}, bf16[1,80,2240]{2,1,0:T(8,128)(2,1)S(1)}, u32[]{:S(2)}, u32[]{:S(2)}) %collective-permute-start.1) | collective-permute-done | bytes 358432 | tf_op jit(solution)/shard_map/ppermute | solution.py:30
  127.9 0.5 maximum_convert_fusion
  128.4 10.0 %fusion.5 = bf16[1,6,80,2240]{3,2,1,0:T(8,128)(2,1)} fusion(f32[2240]{0:T(1024)S(1)} %get-tuple-element.116, f32[2240]{0:T(1024)S(1)} %get-tuple-element.117, f32[2240]{0:T(1024)S(1)} %get-tuple-element.110, f32[2240]{0:T(1024)S(1)} %get-tuple-element.111, f32[2240]{0:T(1024)S(1)} %get-tuple-element.112, f32[2240]{0:T(1024)S(1)} %get-tuple-element.113, ...), kind=kLoop, calls=%fused_computation.18 | loop fusion | flops 45158400 | bytes 23752704 | tf_op jit(solution)/shard_map/reshape | solution.py:78
  (3 shorter events, 0.1 us)
Async XLA Ops:
  6.5 26.9 %reduce-scatter.2.cloned.1.call-start = ((), (), s32[]{:S(2)}) async-start(), calls=%async_computation.1 | async-start | bytes 860160 | tf_op jit(solution)/shard_map/reduce_scatter | solution.py:48
  12.4 6.3 %copy-start = (bf16[480,20,112]{2,1,0:T(8,128)(2,1)S(1)}, bf16[480,20,112]{2,1,0:T(8,128)(2,1)}, u32[]{:S(2)}) copy-start(bf16[480,20,112]{2,1,0:T(8,128)(2,1)} %reshape.47) | copy-start | bytes 6451204
  22.6 65.2 %all-gather.3.cloned.1.call-start = ((), (), s32[]{:S(2)}) async-start(), calls=%async_computation.2 | async-start | bytes 2580480 | tf_op jit(solution)/shard_map/all_gather | solution.py:11
  35.2 7.7 %copy-start.2 = (bf16[10,112,112]{2,1,0:T(8,128)(2,1)S(1)}, bf16[10,112,112]{2,1,0:T(8,128)(2,1)}, u32[]{:S(2)}) copy-start(bf16[10,112,112]{2,1,0:T(8,128)(2,1)} %reduce-scatter.2.cloned.1.call-done) | copy-start | bytes 752644
  112.4 7.0 %copy-start.1 = (bf16[1,6,80,2240]{3,2,1,0:T(8,128)(2,1)S(1)}, bf16[1,6,80,2240]{3,2,1,0:T(8,128)(2,1)}, u32[]{:S(2)}) copy-start(bf16[1,6,80,2240]{3,2,1,0:T(8,128)(2,1)} %param.12) | copy-start | bytes 6451204
  112.4 7.0 %copy-start.5 = (f32[2240]{0:T(1024)S(1)}, f32[2240]{0:T(1024)}, u32[]{:S(2)}) copy-start(f32[2240]{0:T(1024)} %param.13) | copy-start | bytes 26884
  119.4 6.4 %copy-start.3 = (f32[9,2240]{1,0:T(8,128)S(1)}, f32[9,2240]{1,0:T(8,128)}, u32[]{:S(2)}) copy-start(f32[9,2240]{1,0:T(8,128)} %param.15) | copy-start | bytes 241924
  119.4 6.4 %copy-start.4 = (f32[9,2240]{1,0:T(8,128)S(1)}, f32[9,2240]{1,0:T(8,128)}, u32[]{:S(2)}) copy-start(f32[9,2240]{1,0:T(8,128)} %param.14) | copy-start | bytes 241924
  122.3 4.0 %collective-permute-start = (bf16[1,80,2240]{2,1,0:T(8,128)(2,1)S(1)}, bf16[1,80,2240]{2,1,0:T(8,128)(2,1)S(1)}, u32[]{:S(2)}, u32[]{:S(2)}) collective-permute-start(bf16[1,80,2240]{2,1,0:T(8,128)(2,1)S(1)} %get-tuple-element.126), channel_id=1, source_target_pairs={{0,1},{2,3},{4,5},{6,7},{8,9},{10,11},{12,13},{14,15},{16,17},{18,... | collective-permute-start | bytes 1075208 | tf_op jit(solution)/shard_map/ppermute | solution.py:29
  124.4 3.6 %collective-permute-start.1 = (bf16[1,80,2240]{2,1,0:T(8,128)(2,1)S(1)}, bf16[1,80,2240]{2,1,0:T(8,128)(2,1)S(1)}, u32[]{:S(2)}, u32[]{:S(2)}) collective-permute-start(bf16[1,80,2240]{2,1,0:T(8,128)(2,1)S(1)} %get-tuple-element.127), channel_id=1, source_target_pairs={{1,0},{3,2},{5,4},{7,6},{9,8},{11,10},{13,12},{15,14},{17,16},{19,... | collective-permute-start | bytes 1075208 | tf_op jit(solution)/shard_map/ppermute | solution.py:30
Sparse Core Ops, SparseCore 0:
  22.7 10.6 reduce-scatter.1
  35.6 52.1 all-gather.2
where the time goes:
time: 146 us; the launch traced here: 145 us
  waiting for transfers between devices  52.2 us (36%)
  local copies, waits for them, and re-layouts  31.7 us (22%)
  other arithmetic  29.8 us (20%)
  between operations  13.6 us (9%)
  matrix products  9.84 us (7%)
  blocking collectives  4.43 us (3%)
  starting transfers between devices  3.58 us (2%)
    all_gather x1, waiting for transfers between devices, entering(): everything = lax.all_gather(value.astype(jnp.bfloat16), axis)  39.8 us
    reduce_scatter x1, waiting for transfers between devices, on_device(): lax.psum_scatter(partial_value_state.astype(jnp.bfloat16), 'space', scatt...  10.8 us
    reshape x1, other arithmetic, on_device(): return block_out.astype(jnp.bfloat16).reshape(frames, rows, width, dim)  9.99 us
    select_n x8, other arithmetic, step(): return jnp.where(reached, new, before)  9.97 us
    reshape x2, local copies, waits for them, and re-layouts, on_device(): feature_queries = jnp.maximum(queries, 0).reshape(tokens, heads, HEAD_DIM)  7.69 us
    reshape x1, local copies, waits for them, and re-layouts, on_device(): normed = (numerator_sum * scale).reshape(rows, width, dim)  6.99 us
    reshape x1, local copies, waits for them, and re-layouts, on_device(): value_rows = values.reshape(tokens, heads, HEAD_DIM)  6.32 us
    mul x1, local copies, waits for them, and re-layouts, on_device(): normed = (numerator_sum * scale).reshape(rows, width, dim)  6.09 us
  transfers between devices with their start and end apart: 4, of which 3 were waited for; matrix products, arithmetic and copies ran while one was open for 9% of the time, Pallas kernels for 0%

commit v1 on v0

v1 whole, which is shorter than its diff:
```python
import functools

import jax
import jax.numpy as jnp
from jax import lax
from jax.experimental import pallas as pl
from jax.experimental.pallas import tpu as pltpu
from jax.sharding import PartitionSpec as P

HEAD_DIM = 112
LANES = 128
WINDOW = 256
PAD = 8
F32, BF16 = jnp.float32, jnp.bfloat16


def windows(dim):
    out = []
    for lo in range(0, dim, WINDOW):
        w = min(WINDOW, dim - lo)
        h0, h1 = lo // HEAD_DIM, (lo + w - 1) // HEAD_DIM
        ks = HEAD_DIM * h0 // LANES * LANES
        ke = min(dim, -(-HEAD_DIM * (h1 + 1) // LANES) * LANES)
        out.append((lo, w, range(h0, h1 + 1), ks, ke))
    return out


def kernel(
    frames, rows, width, dim,
    q_hbm, k_hbm, v_hbm, r_hbm, gain_ref, vt_ref, gt_ref, o_hbm,
    q, k, v, res, st, pb, rb, ob, yb, pr, ps, vb, numer, sq, mixed, x32, outv,
    load_sem, rs_s, rs_r, ag_s, ag_r, y_s, y_r, z_s, z_r, pv_s, pv_r, halo_s, halo_r, out_sem,
):
    tokens = rows * width
    tiles = st.shape[0]
    per = tiles // 2
    space = lax.axis_index("space")
    frame = lax.axis_index("frame")
    other = 1 - space
    pair, odd = frame // 2, frame % 2
    twin = frame + 1 - 2 * odd
    has_prev = pair > 0
    has_next = pair < frames // 2 - 1

    loads = [
        pltpu.make_async_copy(src, dst, load_sem.at[i])
        for i, (src, dst) in enumerate(((k_hbm, k), (v_hbm, v), (q_hbm, q), (r_hbm, res)))
    ]
    for copy in loads:
        copy.start()

    barrier = pltpu.get_barrier_semaphore()
    pl.semaphore_signal(barrier, inc=1, device_id={"space": other})
    pl.semaphore_signal(barrier, inc=1, device_id={"frame": twin})

    @pl.when(has_prev)
    def _():
        pl.semaphore_signal(barrier, inc=1, device_id={"frame": frame - 2})

    @pl.when(has_next)
    def _():
        pl.semaphore_signal(barrier, inc=1, device_id={"frame": frame + 2})

    x32[...] = jnp.zeros_like(x32)
    st[tiles - 1] = jnp.zeros(st.shape[1:], F32)
    mixed[pl.ds(pl.multiple_of(space * (tokens + width), width), width), :] = jnp.zeros((width, dim), BF16)

    pl.semaphore_wait(barrier, 2 + jnp.where(has_prev, 1, 0) + jnp.where(has_next, 1, 0))

    def to_other(src, dst, tile, send, recv, j):
        return pltpu.make_async_remote_copy(
            src_ref=src.at[tile], dst_ref=dst.at[tile], send_sem=send.at[j], recv_sem=recv.at[j],
            device_id={"space": other},
        )

    def to_frame(src, dst, tile, send, recv, j, target):
        return pltpu.make_async_remote_copy(
            src_ref=src.at[tile], dst_ref=dst.at[tile], send_sem=send.at[j], recv_sem=recv.at[j],
            device_id={"frame": target},
        )

    def head_of(lo, w):
        return (lax.broadcasted_iota(jnp.int32, (HEAD_DIM, w), 1) + lo) // HEAD_DIM

    wins = windows(dim)
    loads[0].wait()
    loads[1].wait()
    order = [i // 2 if i % 2 == 0 else (len(wins) + 1) // 2 + i // 2 for i in range(len(wins))]
    for m in order:
        lo, w, heads, ks, ke = wins[m]
        full = lax.dot_general(
            jnp.maximum(k[:, ks:ke], 0), v[:, lo : lo + w], (((0,), (0,)), ((), ())), preferred_element_type=F32
        )
        owner = head_of(lo, w)
        slab = jnp.zeros((HEAD_DIM, w), F32)
        for h in heads:
            at = HEAD_DIM * h - ks
            slab = jnp.where(owner == h, full[at : at + HEAD_DIM, :], slab)
        for part in range(-(-w // LANES)):
            tile = lo // LANES + part
            wide = min(LANES, w - part * LANES)
            st[tile, :, :wide] = slab[:, part * LANES : part * LANES + wide]
            pb[tile] = st[tile].astype(BF16)

            @pl.when(other == tile // per)
            def _():
                to_other(pb, rb, tile, rs_s, rs_r, tile % per).start()

    def own_step(j, _):
        tile = space * per + j
        to_other(pb, rb, tile, rs_s, rs_r, j).wait_recv()
        total = st[tile] + rb[tile].astype(F32)
        st[tile] = total
        ob[tile] = total.astype(BF16)
        to_frame(ob, yb, tile, y_s, y_r, j, twin).start()
        to_other(ob, ob, tile, ag_s, ag_r, j).start()
        return 0

    lax.fori_loop(0, per, own_step, 0)

    def scan_step(j, _):
        tile = space * per + j
        to_frame(ob, yb, tile, y_s, y_r, j, twin).wait_recv()
        beside = yb[tile].astype(F32)

        @pl.when(has_prev)
        def _():
            to_frame(ps, pr, tile, z_s, z_r, j, frame - 2).wait_recv()

        @pl.when(jnp.logical_not(has_prev))
        def _():
            pr[tile] = jnp.zeros(pr.shape[1:], BF16)

        before = pr[tile].astype(F32)

        @pl.when(has_next)
        def _():
            ps[tile] = (before + (st[tile] + beside)).astype(BF16)
            to_frame(ps, pr, tile, z_s, z_r, j, frame + 2).start()

        vb[tile] = (before + beside * odd.astype(F32)).astype(BF16)
        to_other(vb, vb, tile, pv_s, pv_r, j).start()
        return 0

    lax.fori_loop(0, per, scan_step, 0)

    def arrive_step(j, _):
        tile = other * per + j
        to_other(ob, ob, tile, ag_s, ag_r, j).wait_recv()
        to_other(vb, vb, tile, pv_s, pv_r, j).wait_recv()
        return 0

    lax.fori_loop(0, per, arrive_step, 0)
    loads[2].wait()

    def spread(state, lo, w, heads, ks, ke):
        first = lo // LANES
        slab = jnp.concatenate([state[first + p] for p in range(-(-w // LANES))], axis=1)[:, :w]
        owner = head_of(lo, w)
        pieces = []
        if HEAD_DIM * heads[0] > ks:
            pieces.append(jnp.zeros((HEAD_DIM * heads[0] - ks, w), BF16))
        for h in heads:
            pieces.append(jnp.where(owner == h, slab, jnp.zeros_like(slab)))
        end = HEAD_DIM * (heads[-1] + 1)
        if end < ke:
            pieces.append(jnp.zeros((ke - end, w), BF16))
        return jnp.concatenate(pieces, axis=0)

    for lo, w, heads, ks, ke in wins:
        phi = jnp.maximum(q[:, ks:ke], 0)
        found = jnp.dot(phi, spread(vb, lo, w, heads, ks, ke), preferred_element_type=F32)
        found = found + jnp.dot(phi, spread(ob, lo, w, heads, ks, ke), preferred_element_type=F32)
        numer[:, lo : lo + w] = found
        sq[:, lo : lo + w] = (found * found).astype(BF16)
    loads[3].wait()
    for lo, w, heads, ks, ke in wins:
        from_head = (lax.broadcasted_iota(jnp.int32, (ke - ks, w), 0) + ks) // HEAD_DIM
        to_head = (lax.broadcasted_iota(jnp.int32, (ke - ks, w), 1) + lo) // HEAD_DIM
        same = jnp.where(from_head == to_head, 1.0, 0.0).astype(BF16)
        total = jnp.dot(sq[:, ks:ke], same, preferred_element_type=F32)
        scale = lax.rsqrt(total * (1.0 / HEAD_DIM) + 1e-6)
        normed = numer[:, lo : lo + w] * scale
        value = res[:, lo : lo + w].astype(F32) + normed * gain_ref[:, lo : lo + w]
        mixed[width : width + tokens, lo : lo + w] = value.astype(BF16)

    halo = pltpu.make_async_remote_copy(
        src_ref=mixed.at[pl.ds(pl.multiple_of(width + other * (tokens - width), width), width)],
        dst_ref=mixed.at[pl.ds(pl.multiple_of(space * (tokens + width), width), width)],
        send_sem=halo_s, recv_sem=halo_r, device_id={"space": other},
    )
    halo.start()
    halo.wait()

    step = width + 2 * PAD

    def conv(lo, w):
        at = pl.ds(lo, w)
        for row in range(rows + 2):
            x32[row * step + PAD : row * step + PAD + width, :w] = mixed[row * width : (row + 1) * width, at].astype(F32)
        for row in range(rows):
            cv = jnp.zeros((width, w), F32)
            cg = jnp.zeros((width, w), F32)
            for i in range(3):
                for j in range(3):
                    start = (row + i) * step + PAD - 1 + j
                    x = x32[start : start + width, :w]
                    cv = cv + vt_ref[3 * i + j : 3 * i + j + 1, at] * x
                    cg = cg + gt_ref[3 * i + j : 3 * i + j + 1, at] * x
            centre = (row + 1) * step + PAD
            half = 0.5 * cg
            value = x32[centre : centre + width, :w] + cv * (half + half * jnp.tanh(half))
            outv[row * width : (row + 1) * width, at] = value.astype(BF16)

    whole = dim // LANES

    def conv_step(t, _):
        conv(pl.multiple_of(t * LANES, LANES), LANES)
        return 0

    lax.fori_loop(0, whole, conv_step, 0)
    if dim % LANES:
        conv(whole * LANES, dim % LANES)
    store = pltpu.make_async_copy(outv, o_hbm, out_sem)
    store.start()

    def drain_step(j, _):
        mine, theirs = space * per + j, other * per + j
        to_other(pb, rb, theirs, rs_s, rs_r, j).wait_send()
        to_other(ob, ob, mine, ag_s, ag_r, j).wait_send()
        to_frame(ob, yb, mine, y_s, y_r, j, twin).wait_send()
        to_other(vb, vb, mine, pv_s, pv_r, j).wait_send()

        @pl.when(has_next)
        def _():
            to_frame(ps, pr, mine, z_s, z_r, j, frame + 2).wait_send()

        return 0

    lax.fori_loop(0, per, drain_step, 0)
    store.wait()


def solution(mesh):
    frames = mesh.shape["frame"]

    def on_device(queries, keys, values, residual, attn_gain, value_taps, gate_taps):
        _, rows, width, dim = queries.shape
        tokens = rows * width
        tiles = -(-dim // (2 * LANES)) * 2
        flat = lambda a: a.reshape(tokens, dim)
        anywhere = pl.BlockSpec(memory_space=pl.ANY)
        inside = pl.BlockSpec(memory_space=pltpu.VMEM)
        state = (tiles, HEAD_DIM, LANES)
        sems = pltpu.SemaphoreType.DMA((tiles // 2,))
        out = pl.pallas_call(
            functools.partial(kernel, frames, rows, width, dim),
            out_shape=jax.ShapeDtypeStruct((tokens, dim), BF16),
            in_specs=[anywhere] * 4 + [inside] * 3,
            out_specs=anywhere,
            scratch_shapes=[pltpu.VMEM((tokens, dim), BF16)] * 4
            + [pltpu.VMEM(state, F32)]
            + [pltpu.VMEM(state, BF16)] * 7
            + [
                pltpu.VMEM((tokens, dim), F32),
                pltpu.VMEM((tokens, dim), BF16),
                pltpu.VMEM((tokens + 2 * width, dim), BF16),
                pltpu.VMEM(((rows + 2) * (width + 2 * PAD), LANES), F32),
                pltpu.VMEM((tokens, dim), BF16),
                pltpu.SemaphoreType.DMA((4,)),
            ]
            + [sems] * 10
            + [pltpu.SemaphoreType.DMA] * 3,
            compiler_params=pltpu.CompilerParams(
                collective_id=0, has_side_effects=True, vmem_limit_bytes=60 << 20
            ),
        )(flat(queries), flat(keys), flat(values), flat(residual), attn_gain.reshape(1, dim), value_taps, gate_taps)
        return out.reshape(1, rows, width, dim)

    placed = P(("groups", "frame"), "space", None, None)
    return jax.shard_map(
        on_device,
        mesh=mesh,
        in_specs=(placed,) * 4 + (P(),) * 3,
        out_specs=placed,
        check_vma=False,
    )
```

time: 146 us -> 43.5 us (0.30)
  the two profiles are of different devices: /device:TPU:0 before, /device:TPU:25 now
where the time goes in v1:
time: 43.5 us; the launch traced here: 43.3 us
  Pallas kernels  38.8 us (89%)
  local copies, waits for them, and re-layouts  4.43 us (10%)
    pallas_call x1, Pallas kernels, on_device(): pl.pallas_call(functools.partial(kernel, frames, rows, width, dim), out_s...  38.8 us
    unnamed x1, local copies, waits for them, and re-layouts  3.12 us
    reshape x1, local copies, waits for them, and re-layouts, on_device(): attn_gain.reshape(1, dim)  1.31 us

profile of v1, /device:TPU:25, one launch (start us, length us, event | category | flops | bytes accessed | tf_op | source)
XLA Modules:
  0.0 43.3 jit_solution(16381301224352347496)
XLA Ops:
  0.0 1.3 %reshape.22.gain_ref = f32[1,2240]{1,0:T(1,128)} reshape(f32[2240]{0:T(1024)} %param.11) | data formatting | bytes 17920 | tf_op jit(solution)/shard_map/reshape | solution.py:277
  1.3 38.8 %shard_map.73 = bf16[480,2240]{1,0:T(8,128)(2,1)} custom-call(bf16[480,2240]{1,0:T(8,128)(2,1)} %bitcast.6, bf16[480,2240]{1,0:T(8,128)(2,1)} %bitcast.7, bf16[480,2240]{1,0:T(8,128)(2,1)} %bitcast.8, bf16[480,2240]{1,0:T(8,128)(2,1)} %bitcast.9, f32[1,2240]{1,0:T(1,128)} %reshape.22.gain_ref, f32[9,2240]{1,0:T(8,128)} %vt_ref.1, f32[9,2240]{1,0:T(8,128)} %gt_ref.1), custom_call_target="tpu_custom_call" | custom-call | tf_op jit(solution)/shard_map/pallas_call | solution.py:256
  40.2 3.1 %copy.9 = bf16[1,6,80,2240]{3,2,1,0:T(8,128)(2,1)} copy(bf16[1,6,80,2240]{3,2,1,0:T(8,128)(2,1)} %bitcast.5) | data formatting | bytes 4300800

commit v2 on v1

v2 whole, which is shorter than its diff:
```python
import functools

import jax
import jax.numpy as jnp
from jax import lax
from jax.experimental import pallas as pl
from jax.experimental.pallas import tpu as pltpu
from jax.sharding import PartitionSpec as P

HEAD_DIM = 112
LANES = 128
WINDOW = 256
PAD = 8
PIECE = 768
BLOCK = 384
LAG = 1
AHEAD = 2
F32, BF16 = jnp.float32, jnp.bfloat16


def windows(dim):
    out = []
    for lo in range(0, dim, WINDOW):
        w = min(WINDOW, dim - lo)
        h0, h1 = lo // HEAD_DIM, (lo + w - 1) // HEAD_DIM
        ks = HEAD_DIM * h0 // LANES * LANES
        ke = min(dim, -(-HEAD_DIM * (h1 + 1) // LANES) * LANES)
        out.append((lo, w, range(h0, h1 + 1), ks, ke))
    return out


def mix_kernel(
    frames, rows, width, dim,
    q_hbm, k_hbm, v_hbm, r_hbm, gain_ref, o_hbm,
    q, k, v, res, st, pb, rb, ob, yb, pr, ps, vb, numer, sq, mixed,
    kv_sem, load_sem, edge_s, edge_r, rs_s, rs_r, ag_s, ag_r, y_s, y_r, z_s, z_r, pv_s, pv_r, out_sem,
):
    tokens = rows * width
    tiles = st.shape[0]
    space = lax.axis_index("space")
    frame = lax.axis_index("frame")
    other = 1 - space
    pair, odd = frame // 2, frame % 2
    twin = frame + 1 - 2 * odd
    has_prev = pair > 0
    has_next = pair < frames // 2 - 1
    wins = windows(dim)
    steps = len(wins)

    cuts = list(range(0, dim, PIECE)) + [dim]
    kv_loads = []
    for i, (lo, hi) in enumerate(zip(cuts, cuts[1:])):
        kv_loads.append(
            [
                pltpu.make_async_copy(src.at[:, lo:hi], dst.at[:, lo:hi], kv_sem.at[c, i])
                for c, (src, dst) in enumerate(((k_hbm, k), (v_hbm, v)))
            ]
        )
    loads = [
        pltpu.make_async_copy(src, dst.at[0:tokens], load_sem.at[i]) for i, (src, dst) in enumerate(((q_hbm, q), (r_hbm, res)))
    ]
    for copies in kv_loads:
        for copy in copies:
            copy.start()
    for copy in loads:
        copy.start()

    barrier = pltpu.get_barrier_semaphore()
    pl.semaphore_signal(barrier, inc=1, device_id={"space": other})
    pl.semaphore_signal(barrier, inc=1, device_id={"frame": twin})

    @pl.when(has_prev)
    def _():
        pl.semaphore_signal(barrier, inc=1, device_id={"frame": frame - 2})

    @pl.when(has_next)
    def _():
        pl.semaphore_signal(barrier, inc=1, device_id={"frame": frame + 2})

    st[tiles - 1] = jnp.zeros(st.shape[1:], F32)
    mixed[pl.ds(pl.multiple_of(space * (tokens + width), width), width), :] = jnp.zeros((width, dim), BF16)

    pl.semaphore_wait(barrier, 2 + jnp.where(has_prev, 1, 0) + jnp.where(has_next, 1, 0))

    def to_other(src, dst, tile, send, recv, j):
        return pltpu.make_async_remote_copy(
            src_ref=src.at[tile], dst_ref=dst.at[tile], send_sem=send.at[j], recv_sem=recv.at[j],
            device_id={"space": other},
        )

    def to_frame(src, dst, tile, send, recv, j, target):
        return pltpu.make_async_remote_copy(
            src_ref=src.at[tile], dst_ref=dst.at[tile], send_sem=send.at[j], recv_sem=recv.at[j],
            device_id={"frame": target},
        )

    edges = [
        pltpu.make_async_remote_copy(
            src_ref=src.at[pl.ds(pl.multiple_of(other * (tokens - width), width), width)],
            dst_ref=dst.at[tokens : tokens + width],
            send_sem=edge_s.at[i], recv_sem=edge_r.at[i], device_id={"space": other},
        )
        for i, (src, dst) in enumerate(((q_hbm, q), (r_hbm, res)))
    ]

    def head_of(lo, w):
        return (lax.broadcasted_iota(jnp.int32, (HEAD_DIM, w), 1) + lo) // HEAD_DIM

    def own_step(j):
        tile = 2 * j + space
        to_other(pb, rb, tile, rs_s, rs_r, j).wait_recv()
        total = st[tile] + rb[tile].astype(F32)
        st[tile] = total
        ob[tile] = total.astype(BF16)
        to_frame(ob, yb, tile, y_s, y_r, j, twin).start()
        to_other(ob, ob, tile, ag_s, ag_r, j).start()

    ready = 0
    for m in range(steps):
        lo, w, heads, ks, ke = wins[m]
        while cuts[ready] < ke:
            for copy in kv_loads[ready]:
                copy.wait()
            ready += 1
        full = lax.dot_general(
            jnp.maximum(k[:, ks:ke], 0), v[:, lo : lo + w], (((0,), (0,)), ((), ())), preferred_element_type=F32
        )
        owner = head_of(lo, w)
        slab = jnp.zeros((HEAD_DIM, w), F32)
        for h in heads:
            at = HEAD_DIM * h - ks
            slab = jnp.where(owner == h, full[at : at + HEAD_DIM, :], slab)
        for part in range(-(-w // LANES)):
            tile = lo // LANES + part
            wide = min(LANES, w - part * LANES)
            st[tile, :, :wide] = slab[:, part * LANES : part * LANES + wide]
            pb[tile] = st[tile].astype(BF16)
        to_other(pb, rb, 2 * m + other, rs_s, rs_r, m).start()
        if m >= LAG:
            own_step(m - LAG)
    for m in range(max(0, steps - LAG), steps):
        own_step(m)
    for copy in edges:
        copy.start()

    def scan_step(j):
        tile = 2 * j + space
        to_frame(ob, yb, tile, y_s, y_r, j, twin).wait_recv()
        beside = yb[tile].astype(F32)

        @pl.when(has_prev)
        def _():
            to_frame(ps, pr, tile, z_s, z_r, j, frame - 2).wait_recv()

        @pl.when(jnp.logical_not(has_prev))
        def _():
            pr[tile] = jnp.zeros(pr.shape[1:], BF16)

        before = pr[tile].astype(F32)

        @pl.when(has_next)
        def _():
            ps[tile] = (before + (st[tile] + beside)).astype(BF16)
            to_frame(ps, pr, tile, z_s, z_r, j, frame + 2).start()

        vb[tile] = (before + beside * odd.astype(F32)).astype(BF16)
        to_other(vb, vb, tile, pv_s, pv_r, j).start()

    @pl.when(has_next)
    def _():
        def relay(j, _):
            scan_step(j)
            return 0

        lax.fori_loop(0, steps, relay, 0)

    def last_in_chain(first, end):
        @pl.when(jnp.logical_not(has_next))
        def _():
            for j in range(first, min(end, steps)):
                scan_step(j)

    def spread(state, lo, w, heads, ks, ke):
        first = lo // LANES
        slab = jnp.concatenate([state[first + p] for p in range(-(-w // LANES))], axis=1)[:, :w]
        owner = head_of(lo, w)
        pieces = []
        if HEAD_DIM * heads[0] > ks:
            pieces.append(jnp.zeros((HEAD_DIM * heads[0] - ks, w), BF16))
        for h in heads:
            pieces.append(jnp.where(owner == h, slab, jnp.zeros_like(slab)))
        end = HEAD_DIM * (heads[-1] + 1)
        if end < ke:
            pieces.append(jnp.zeros((ke - end, w), BF16))
        return jnp.concatenate(pieces, axis=0)

    for copy in loads:
        copy.wait()
    for copy in edges:
        copy.wait_recv()

    def numer_step(m):
        lo, w, heads, ks, ke = wins[m]
        tile = 2 * m + other
        to_other(ob, ob, tile, ag_s, ag_r, m).wait_recv()
        to_other(vb, vb, tile, pv_s, pv_r, m).wait_recv()
        phi = jnp.maximum(q[:, ks:ke], 0)
        found = jnp.dot(phi, spread(vb, lo, w, heads, ks, ke), preferred_element_type=F32)
        found = found + jnp.dot(phi, spread(ob, lo, w, heads, ks, ke), preferred_element_type=F32)
        numer[:, lo : lo + w] = found
        sq[:, lo : lo + w] = (found * found).astype(BF16)

    far = pl.ds(pl.multiple_of((1 - space) * (tokens + width), width), width)
    stores = []

    def mixed_step(m):
        lo, w, heads, ks, ke = wins[m]
        from_head = (lax.broadcasted_iota(jnp.int32, (ke - ks, w), 0) + ks) // HEAD_DIM
        to_head = (lax.broadcasted_iota(jnp.int32, (ke - ks, w), 1) + lo) // HEAD_DIM
        same = jnp.where(from_head == to_head, 1.0, 0.0).astype(BF16)
        total = jnp.dot(sq[:, ks:ke], same, preferred_element_type=F32)
        scale = lax.rsqrt(total * (1.0 / HEAD_DIM) + 1e-6)
        normed = numer[:, lo : lo + w] * scale
        value = (res[:, lo : lo + w].astype(F32) + normed * gain_ref[lo : lo + w].reshape(1, w)).astype(BF16)
        mixed[width : width + tokens, lo : lo + w] = value[:tokens]
        mixed[far, lo : lo + w] = value[tokens:]
        store = pltpu.make_async_copy(mixed.at[:, lo : lo + w], o_hbm.at[:, lo : lo + w], out_sem.at[m])
        store.start()
        stores.append(store)

    last_in_chain(0, AHEAD)
    for m in range(steps):
        last_in_chain(m + AHEAD, m + AHEAD + 1)
        numer_step(m)
        if m > 0:
            mixed_step(m - 1)
    mixed_step(steps - 1)

    for copy in edges:
        copy.wait_send()

    def drain_step(j, _):
        mine, theirs = 2 * j + space, 2 * j + other
        to_other(pb, rb, theirs, rs_s, rs_r, j).wait_send()
        to_other(ob, ob, mine, ag_s, ag_r, j).wait_send()
        to_frame(ob, yb, mine, y_s, y_r, j, twin).wait_send()
        to_other(vb, vb, mine, pv_s, pv_r, j).wait_send()

        @pl.when(has_next)
        def _():
            to_frame(ps, pr, mine, z_s, z_r, j, frame + 2).wait_send()

        return 0

    lax.fori_loop(0, steps, drain_step, 0)
    for store in stores:
        store.wait()


def conv_kernel(rows, width, m_ref, vt_ref, gt_ref, o_ref, x32):
    step = width + 2 * PAD

    @pl.when(pl.program_id(0) == 0)
    def _():
        x32[...] = jnp.zeros_like(x32)

    def tile_step(t, _):
        at = pl.ds(pl.multiple_of(t * LANES, LANES), LANES)
        for row in range(rows + 2):
            x32[row * step + PAD : row * step + PAD + width, :] = m_ref[row * width : (row + 1) * width, at].astype(F32)
        for row in range(rows):
            cv = jnp.zeros((width, LANES), F32)
            cg = jnp.zeros((width, LANES), F32)
            for i in range(3):
                for j in range(3):
                    start = (row + i) * step + PAD - 1 + j
                    x = x32[start : start + width, :]
                    cv = cv + vt_ref[3 * i + j : 3 * i + j + 1, at] * x
                    cg = cg + gt_ref[3 * i + j : 3 * i + j + 1, at] * x
            centre = (row + 1) * step + PAD
            half = 0.5 * cg
            value = x32[centre : centre + width, :] + cv * (half + half * jnp.tanh(half))
            o_ref[row * width : (row + 1) * width, at] = value.astype(BF16)
        return 0

    lax.fori_loop(0, o_ref.shape[1] // LANES, tile_step, 0)


def solution(mesh):
    frames = mesh.shape["frame"]

    def on_device(queries, keys, values, residual, attn_gain, value_taps, gate_taps):
        _, rows, width, dim = queries.shape
        tokens = rows * width
        steps = -(-dim // WINDOW)
        flat = lambda a: a.reshape(tokens, dim)
        anywhere = pl.BlockSpec(memory_space=pl.ANY)
        state = (2 * steps, HEAD_DIM, LANES)
        sems = pltpu.SemaphoreType.DMA((steps,))
        two = pltpu.SemaphoreType.DMA((2,))
        ext = tokens + width
        mixed = pl.pallas_call(
            functools.partial(mix_kernel, frames, rows, width, dim),
            out_shape=jax.ShapeDtypeStruct((tokens + 2 * width, dim), BF16),
            in_specs=[anywhere] * 4 + [pl.BlockSpec(memory_space=pltpu.VMEM)],
            out_specs=anywhere,
            scratch_shapes=[
                pltpu.VMEM((ext, dim), BF16),
                pltpu.VMEM((tokens, dim), BF16),
                pltpu.VMEM((tokens, dim), BF16),
                pltpu.VMEM((ext, dim), BF16),
                pltpu.VMEM(state, F32),
            ]
            + [pltpu.VMEM(state, BF16)] * 7
            + [
                pltpu.VMEM((ext, dim), F32),
                pltpu.VMEM((ext, dim), BF16),
                pltpu.VMEM((tokens + 2 * width, dim), BF16),
                pltpu.SemaphoreType.DMA((2, -(-dim // PIECE))),
                two,
                two,
                two,
            ]
            + [sems] * 11,
            compiler_params=pltpu.CompilerParams(collective_id=0, has_side_effects=True, vmem_limit_bytes=56 << 20),
        )(flat(queries), flat(keys), flat(values), flat(residual), attn_gain, )
        out = pl.pallas_call(
            functools.partial(conv_kernel, rows, width),
            out_shape=jax.ShapeDtypeStruct((tokens, dim), BF16),
            grid=(-(-dim // BLOCK),),
            in_specs=[
                pl.BlockSpec((tokens + 2 * width, BLOCK), lambda c: (0, c)),
                pl.BlockSpec((9, BLOCK), lambda c: (0, c)),
                pl.BlockSpec((9, BLOCK), lambda c: (0, c)),
            ],
            out_specs=pl.BlockSpec((tokens, BLOCK), lambda c: (0, c)),
            scratch_shapes=[pltpu.VMEM(((rows + 2) * (width + 2 * PAD), LANES), F32)],
        )(mixed, value_taps, gate_taps)
        return out.reshape(1, rows, width, dim)

    placed = P(("groups", "frame"), "space", None, None)
    return jax.shard_map(
        on_device,
        mesh=mesh,
        in_specs=(placed,) * 4 + (P(),) * 3,
        out_specs=placed,
        check_vma=False,
    )
```

time: 43.5 us -> 37.7 us (0.87)
  the two profiles are of different devices: /device:TPU:25 before, /device:TPU:16 now
where the time goes in v2:
time: 37.7 us; the launch traced here: 37.4 us
  Pallas kernels  37.4 us (99%)
    pallas_call x1, Pallas kernels, on_device(): pl.pallas_call(functools.partial(mix_kernel, frames, rows, width, dim), o...  28.5 us
    pallas_call x1, Pallas kernels, on_device(): pl.pallas_call(functools.partial(conv_kernel, rows, width), out_shape=jax...  8.88 us

profile of v2, /device:TPU:16, one launch (start us, length us, event | category | flops | bytes accessed | tf_op | source)
XLA Modules:
  0.0 37.4 jit_solution(4292426886409048365)
XLA Ops:
  0.0 28.5 %shard_map.73.m_ref = bf16[640,2240]{1,0:T(8,128)(2,1)} custom-call(bf16[480,2240]{1,0:T(8,128)(2,1)} %bitcast.5, bf16[480,2240]{1,0:T(8,128)(2,1)} %bitcast.6, bf16[480,2240]{1,0:T(8,128)(2,1)} %bitcast.7, bf16[480,2240]{1,0:T(8,128)(2,1)} %bitcast.8, f32[2240]{0:T(1024)} %gain_ref.1), custom_call_target="tpu_custom_call" | custom-call | tf_op jit(solution)/shard_map/pallas_call | solution.py:302
  28.5 8.9 %shard_map.74 = bf16[480,2240]{1,0:T(8,128)(2,1)} custom-call(bf16[640,2240]{1,0:T(8,128)(2,1)} %shard_map.73.m_ref, f32[9,2240]{1,0:T(8,128)} %vt_ref.1, f32[9,2240]{1,0:T(8,128)} %gt_ref.1), custom_call_target="tpu_custom_call" | custom-call | tf_op jit(solution)/shard_map/pallas_call | solution.py:327

commit v3 on v2

--- a/solution.py
+++ b/solution.py
@@ -13,7 +13,7 @@
 PAD = 8
 PIECE = 768
 BLOCK = 384
-LAG = 1
+LAG = 2
 AHEAD = 2
 F32, BF16 = jnp.float32, jnp.bfloat16
 
@@ -259,6 +259,7 @@
 
 def conv_kernel(rows, width, m_ref, vt_ref, gt_ref, o_ref, x32):
     step = width + 2 * PAD
+    part = 16
 
     @pl.when(pl.program_id(0) == 0)
     def _():
@@ -268,19 +269,22 @@
         at = pl.ds(pl.multiple_of(t * LANES, LANES), LANES)
         for row in range(rows + 2):
             x32[row * step + PAD : row * step + PAD + width, :] = m_ref[row * width : (row + 1) * width, at].astype(F32)
+        taps = [
+            (jnp.broadcast_to(vt_ref[n : n + 1, at], (part, LANES)), jnp.broadcast_to(gt_ref[n : n + 1, at], (part, LANES)))
+            for n in range(9)
+        ]
         for row in range(rows):
-            cv = jnp.zeros((width, LANES), F32)
-            cg = jnp.zeros((width, LANES), F32)
-            for i in range(3):
-                for j in range(3):
-                    start = (row + i) * step + PAD - 1 + j
-                    x = x32[start : start + width, :]
-                    cv = cv + vt_ref[3 * i + j : 3 * i + j + 1, at] * x
-                    cg = cg + gt_ref[3 * i + j : 3 * i + j + 1, at] * x
-            centre = (row + 1) * step + PAD
-            half = 0.5 * cg
-            value = x32[centre : centre + width, :] + cv * (half + half * jnp.tanh(half))
-            o_ref[row * width : (row + 1) * width, at] = value.astype(BF16)
+            for off in range(0, width, part):
+                cv, cg = None, None
+                for n in range(9):
+                    start = (row + n // 3) * step + PAD - 1 + n % 3 + off
+                    x = x32[start : start + part, :]
+                    cv = taps[n][0] * x if cv is None else cv + taps[n][0] * x
+                    cg = taps[n][1] * x if cg is None else cg + taps[n][1] * x
+                centre = (row + 1) * step + PAD + off
+                half = 0.5 * cg
+                value = x32[centre : centre + part, :] + cv * (half + half * jnp.tanh(half))
+                o_ref[row * width + off : row * width + off + part, at] = value.astype(BF16)
         return 0
 
     lax.fori_loop(0, o_ref.shape[1] // LANES, tile_step, 0)

time: 37.7 us -> 35.7 us (0.947)
  the two profiles are of different devices: /device:TPU:16 before, /device:TPU:25 now
where the time goes in v3:
time: 35.7 us; the launch traced here: 35.1 us
  Pallas kernels  35.1 us (98%)
    pallas_call x1, Pallas kernels, on_device(): pl.pallas_call(functools.partial(mix_kernel, frames, rows, width, dim), o...  26.4 us
    pallas_call x1, Pallas kernels, on_device(): pl.pallas_call(functools.partial(conv_kernel, rows, width), out_shape=jax...  8.69 us

profile of v3, /device:TPU:25, one launch (start us, length us, event | category | flops | bytes accessed | tf_op | source)
XLA Modules:
  0.0 35.1 jit_solution(16892526458199071350)
XLA Ops:
  0.0 26.4 %shard_map.73.m_ref = bf16[640,2240]{1,0:T(8,128)(2,1)} custom-call(bf16[480,2240]{1,0:T(8,128)(2,1)} %bitcast.5, bf16[480,2240]{1,0:T(8,128)(2,1)} %bitcast.6, bf16[480,2240]{1,0:T(8,128)(2,1)} %bitcast.7, bf16[480,2240]{1,0:T(8,128)(2,1)} %bitcast.8, f32[2240]{0:T(1024)} %gain_ref.1), custom_call_target="tpu_custom_call" | custom-call | tf_op jit(solution)/shard_map/pallas_call | solution.py:306
  26.4 8.7 %shard_map.74 = bf16[480,2240]{1,0:T(8,128)(2,1)} custom-call(bf16[640,2240]{1,0:T(8,128)(2,1)} %shard_map.73.m_ref, f32[9,2240]{1,0:T(8,128)} %vt_ref.1, f32[9,2240]{1,0:T(8,128)} %gt_ref.1), custom_call_target="tpu_custom_call" | custom-call | tf_op jit(solution)/shard_map/pallas_call | solution.py:331
